TPU v7x, 512 devices: a whole 4x8x8 slice. The times are simulated.
512 devices in a mesh: row: 16 (over z, core), col: 32 (over x, y).
Axes of the slice: x: 4, y: 8, z: 8, core: 2. Of those that a mesh axis runs over, the one named last changes fastest.
Arguments:
- matrix: float32 [8192, 8192], P('row', 'col'), may hold values from -6 to 6
- inverses: float32 [4, 256, 256], P(None, 'row'), may hold values from -0.01171875 to 0.01171875
- pivots: int32 [4], replicated, may hold values from 0 to 31, as said below
- row_mask: int32 [4, 32], replicated, may hold values 0 or 1
- col_mask: int32 [4, 32], replicated, may hold values 0 or 1
Outputs:
- factored: float32 [8192, 8192], P('row', 'col')
Inputs may be any that keep to these rules, and one draw needn't show every extreme that they name: `pivots`: 4 distinct block indices; 0 and 31 are always among them.
All inputs are finite; a program needn't handle non-finite values.
Results may differ from a plain program's by a relative error of at most 0.0001.
Values sent between devices are 32-bit elements; how exact they have to be, the bound alone decides.
A program may use at most 64 MiB of HBM per device.

v0:
```python
import jax
import jax.numpy as jnp
from jax import lax
from jax.sharding import PartitionSpec as P


def from_root(block, axis, source):
    block = jnp.where(lax.axis_index(axis) == source, block, jnp.zeros_like(block))
    return lax.psum(block, axis)


def on_device(matrix, inverses, pivots, row_mask, col_mask):
    highest = lax.Precision.HIGHEST
    block_width = inverses.shape[2]
    panel_count = inverses.shape[0]
    row_blocks = matrix.shape[0] // block_width
    col_blocks = matrix.shape[1] // block_width
    row_id = lax.axis_index("row")
    col_id = lax.axis_index("col")
    my_rows = row_id * row_blocks + jnp.arange(row_blocks, dtype=jnp.int32)
    my_cols = col_id * col_blocks + jnp.arange(col_blocks, dtype=jnp.int32)
    rows_done = jnp.zeros((row_blocks,), jnp.float32)
    cols_done = jnp.zeros((col_blocks,), jnp.float32)
    anchor = jnp.zeros((), jnp.int32)
    full_inverse = lax.all_gather(inverses, "row", axis=1, tiled=True)
    current = matrix
    carried = None
    for step in range(panel_count):
        pivot_block = pivots[step]
        col_root = pivot_block // col_blocks
        local_col = jnp.clip(pivot_block - col_id * col_blocks, 0, col_blocks - 1)
        column_piece = current
        panel_cols = from_root(column_piece, "col", col_root)
        row_root = pivot_block // row_blocks
        local_row = jnp.clip(pivot_block - row_id * row_blocks, 0, row_blocks - 1)
        row_piece = lax.dynamic_slice(
            current, (local_row * block_width, anchor), (block_width, col_blocks * block_width)
        )
        raw_row = from_root(row_piece, "row", row_root)
        solved = jnp.dot(
            full_inverse[step], raw_row, precision=highest, preferred_element_type=jnp.float32
        )
        keep_cols = jnp.repeat(1.0 - cols_done, block_width)
        is_owner = row_root == row_id
        new_row = jnp.where((keep_cols[None, :] > 0.5) & is_owner, solved, row_piece)
        current = lax.dynamic_update_slice(current, new_row, (local_row * block_width, anchor))
        rows_done = jnp.maximum(rows_done, (my_rows == pivot_block).astype(jnp.float32))
        cols_done = jnp.maximum(cols_done, (my_cols == pivot_block).astype(jnp.float32))
        row_bits = lax.dynamic_slice_in_dim(row_mask[step], row_id * row_blocks, row_blocks).astype(
            jnp.float32
        )
        col_bits = lax.dynamic_slice_in_dim(col_mask[step], col_id * col_blocks, col_blocks).astype(
            jnp.float32
        )
        row_factor = jnp.repeat(row_bits * (1.0 - rows_done), block_width)
        col_factor = jnp.repeat(col_bits * (1.0 - cols_done), block_width)
        left_part = panel_cols * row_factor[:, None]
        right_part = solved * col_factor[None, :]
        carried = None
        current = current - jnp.dot(
            left_part, right_part, precision=highest, preferred_element_type=jnp.float32
        )
    return current


def solution(mesh):
    in_specs = (P("row", "col"), P(None, "row", None), P(), P(), P())
    out_specs = P("row", "col")
    return jax.shard_map(
        on_device, mesh=mesh, in_specs=in_specs, out_specs=out_specs, check_vma=False
    )
```

profile of v0, /device:TPU:1, one launch (start us, length us, event | category | flops | bytes accessed | tf_op | source)
XLA Modules:
  0.0 1184.2 jit_solution(10636890682832242617)
XLA Ops:
  6.5 0.7 copy-done.1
  7.2 0.7 fusion.35
  11.3 1.2 copy.7
  12.5 0.8 dynamic-slice_select_fusion.3
  13.3 0.0 all-gather.2.cloned.1.call-start
  13.4 0.7 all-gather.2.cloned.1.call-update
  14.8 0.8 broadcast_select_fusion.3
  15.7 0.0 all-reduce.13.cloned.1.call-start
  15.7 0.6 copy-done.2
  16.3 0.7 fusion.24
  17.1 0.1 broadcast_bitcast_fusion.3
  21.3 0.7 copy-done.3
  21.9 0.6 fusion.36
  23.2 112.0 %all-reduce.9.cloned.1.call-done = f32[256,256]{0,1:T(8,128)} async-done(((f32[256,256]{0,1:T(8,128)}), f32[256,256]{0,1:T(8,128)}) %all-reduce.9.cloned.1.call-update) | async-done | bytes 262160 | tf_op jit(solution)/shard_map/psum | solution.py:9
  135.2 44.3 %all-gather.2.cloned.1.call-done = f32[4,256,256]{2,1,0:T(8,128)} async-done(((f32[4,16,256]{2,1,0:T(8,128)}), f32[4,256,256]{2,1,0:T(8,128)}) %all-gather.2.cloned.1.call-update) | async-done | bytes 1048592 | tf_op jit(solution)/shard_map/all_gather | solution.py:25
  179.5 1.4 select_dynamic-update-slice_fusion.3
  181.0 154.7 %all-reduce.11.cloned.1.call-done = f32[512,256]{0,1:T(8,128)} async-done(((f32[512,256]{0,1:T(8,128)}), f32[512,256]{0,1:T(8,128)}) %all-reduce.11.cloned.1.call-update) | async-done | bytes 524304 | tf_op jit(solution)/shard_map/psum | solution.py:9
  335.7 2.5 broadcast_select_fusion.2
  338.2 0.8 dynamic-slice_select_fusion.2
  339.0 0.5 all-reduce.15.cloned.1.call-update
  339.6 1.3 fusion.27
  344.9 0.1 broadcast_bitcast_fusion.2
  344.9 0.6 fusion.37
  346.2 111.0 %all-reduce.13.cloned.1.call-done = f32[256,256]{0,1:T(8,128)} async-done(((f32[256,256]{0,1:T(8,128)}), f32[256,256]{0,1:T(8,128)}) %all-reduce.13.cloned.1.call-update) | async-done | bytes 262160 | tf_op jit(solution)/shard_map/psum | solution.py:9
  457.3 1.4 select_dynamic-update-slice_fusion.2
  458.6 156.7 %all-reduce.15.cloned.1.call-done = f32[512,256]{0,1:T(8,128)} async-done(((f32[512,256]{0,1:T(8,128)}), f32[512,256]{0,1:T(8,128)}) %all-reduce.15.cloned.1.call-update) | async-done | bytes 524304 | tf_op jit(solution)/shard_map/psum | solution.py:9
  615.4 2.5 broadcast_select_fusion.1
  617.9 0.7 dynamic-slice_select_fusion.1
  618.6 0.0 all-reduce.19.cloned.1.call-start
  618.7 0.7 all-reduce.19.cloned.1.call-update
  619.4 1.9 fusion.30
  626.0 0.1 broadcast_bitcast_fusion.1
  626.1 0.6 fusion.38
  627.2 109.7 %all-reduce.17.cloned.1.call-done = f32[256,256]{0,1:T(8,128)} async-done(((f32[256,256]{0,1:T(8,128)}), f32[256,256]{0,1:T(8,128)}) %all-reduce.17.cloned.1.call-update) | async-done | bytes 262160 | tf_op jit(solution)/shard_map/psum | solution.py:9
  736.9 1.4 select_dynamic-update-slice_fusion.1
  738.3 156.9 %all-reduce.19.cloned.1.call-done = f32[512,256]{0,1:T(8,128)} async-done(((f32[512,256]{0,1:T(8,128)}), f32[512,256]{0,1:T(8,128)}) %all-reduce.19.cloned.1.call-update) | async-done | bytes 524304 | tf_op jit(solution)/shard_map/psum | solution.py:9
  895.2 2.5 broadcast_select_fusion
  897.7 0.7 dynamic-slice_select_fusion
  898.4 0.0 all-reduce.23.cloned.1.call-start
  898.5 0.7 all-reduce.23.cloned.1.call-update
  899.2 2.6 fusion.21
  902.4 0.1 broadcast_bitcast_fusion
  902.5 0.6 fusion.39
  903.7 113.1 %all-reduce.21.cloned.1.call-done = f32[256,256]{0,1:T(8,128)} async-done(((f32[256,256]{0,1:T(8,128)}), f32[256,256]{0,1:T(8,128)}) %all-reduce.21.cloned.1.call-update) | async-done | bytes 262160 | tf_op jit(solution)/shard_map/psum | solution.py:9
  1016.7 1.4 select_dynamic-update-slice_fusion
  1018.1 156.9 %all-reduce.23.cloned.1.call-done = f32[512,256]{0,1:T(8,128)} async-done(((f32[512,256]{0,1:T(8,128)}), f32[512,256]{0,1:T(8,128)}) %all-reduce.23.cloned.1.call-update) | async-done | bytes 524304 | tf_op jit(solution)/shard_map/psum | solution.py:9
  1175.0 1.7 convolution_subtract_fusion
  1176.7 1.0 copy.13
  (21 shorter events, 0.3 us)
Async XLA Ops:
  6.5 0.7 copy-start.1
  6.5 128.6 %all-reduce.9.cloned.1.call-start = ((), (), s32[]{:S(2)}) async-start(), calls=%async_computation | async-start | bytes 524288 | tf_op jit(solution)/shard_map/psum | solution.py:9
  13.3 166.2 %all-gather.2.cloned.1.call-start = ((), (), s32[]{:S(2)}) async-start(), calls=%async_computation.1 | async-start | bytes 1114112 | tf_op jit(solution)/shard_map/all_gather | solution.py:25
  14.1 321.6 %all-reduce.11.cloned.1.call-start = ((), (), s32[]{:S(2)}) async-start(), calls=%async_computation.2 | async-start | bytes 1048576 | tf_op jit(solution)/shard_map/psum | solution.py:9
  15.6 0.7 copy-start.2
  15.7 441.6 %all-reduce.13.cloned.1.call-start = ((), (), s32[]{:S(2)}) async-start(), calls=%async_computation.3 | async-start | bytes 524288 | tf_op jit(solution)/shard_map/psum | solution.py:9
  21.2 0.7 copy-start.3
  338.2 119.1 %copy-start = (f32[4,256,256]{2,1,0:T(8,128)S(1)}, f32[4,256,256]{2,1,0:T(8,128)}, u32[]{:S(2)}) copy-start(f32[4,256,256]{2,1,0:T(8,128)} %all-gather.2.cloned.1.call-done) | copy-start | bytes 3145732
  339.0 276.4 %all-reduce.15.cloned.1.call-start = ((), (), s32[]{:S(2)}) async-start(), calls=%async_computation.4 | async-start | bytes 1048576 | tf_op jit(solution)/shard_map/psum | solution.py:9
  339.5 397.4 %all-reduce.17.cloned.1.call-start = ((), (), s32[]{:S(2)}) async-start(), calls=%async_computation.5 | async-start | bytes 524288 | tf_op jit(solution)/shard_map/psum | solution.py:9
  618.6 276.6 %all-reduce.19.cloned.1.call-start = ((), (), s32[]{:S(2)}) async-start(), calls=%async_computation.6 | async-start | bytes 1048576 | tf_op jit(solution)/shard_map/psum | solution.py:9
  619.4 397.4 %all-reduce.21.cloned.1.call-start = ((), (), s32[]{:S(2)}) async-start(), calls=%async_computation.7 | async-start | bytes 524288 | tf_op jit(solution)/shard_map/psum | solution.py:9
  898.4 276.6 %all-reduce.23.cloned.1.call-start = ((), (), s32[]{:S(2)}) async-start(), calls=%async_computation.8 | async-start | bytes 1048576 | tf_op jit(solution)/shard_map/psum | solution.py:9
Sparse Core Ops, SparseCore 0:
  13.4 121.7 all-reduce.8
  137.3 42.1 all-gather.1
  182.9 152.7 all-reduce.10
  339.1 118.1 all-reduce.12
  460.5 154.8 all-reduce.14
  618.7 118.1 all-reduce.16
  740.3 154.8 all-reduce.18
  898.5 118.1 all-reduce.20
  1020.1 154.8 all-reduce.22
where the time goes:
time: 1190 us; the launch traced here: 1180 us
  waiting for transfers between devices  1120 us (94%)
  between operations  33.3 us (3%)
  matrix products  14.7 us (1%)
  other arithmetic  12.7 us (1%)
    psum x8, waiting for transfers between devices, from_root(): return lax.psum(block, axis)  1070 us
    all_gather x1, waiting for transfers between devices, on_device(): full_inverse = lax.all_gather(inverses, 'row', axis=1, tiled=True)  44.3 us
  transfers between devices with their start and end apart: 9, of which 9 were waited for; matrix products, arithmetic and copies ran while one was open for 1% of the time, Pallas kernels for 0%

commit v1 on v0

v1 whole, which is shorter than its diff:
```python
import functools

import jax
import jax.numpy as jnp
from jax import lax
from jax.experimental import pallas as pl
from jax.experimental.pallas import tpu as pltpu
from jax.sharding import PartitionSpec as P

MESH = pl.DeviceIdType.MESH
F32 = jnp.float32
BF16 = jnp.bfloat16


class Sems:
    def __init__(self, send, recv):
        self.send, self.recv, self.used = send, recv, 0

    def take(self, count=1):
        first = self.used
        self.used += count
        return first

    def copy(self, src, dst, device, index):
        return pltpu.make_async_remote_copy(
            src_ref=src,
            dst_ref=dst,
            send_sem=self.send.at[index],
            recv_sem=self.recv.at[index],
            device_id=device,
            device_id_type=MESH,
        )


class Ring:
    def __init__(self, sems, n, me, view, right, left, first=None):
        self.n, self.steps = n, n // 2
        self.down, self.up = [], []
        for s in range(self.steps):
            slot = lax.rem(me - s + n, n)
            src = first if s == 0 and first is not None else view(slot)
            self.down.append(sems.copy(src, view(slot), right, sems.take()))
            if s < n - 1 - self.steps:
                slot = lax.rem(me + s, n)
                src = first if s == 0 and first is not None else view(slot)
                self.up.append(sems.copy(src, view(slot), left, sems.take()))

    def start(self, s):
        for way in (self.down, self.up):
            if s < len(way):
                way[s].start()

    def arrive(self, s):
        for way in (self.down, self.up):
            if s < len(way):
                way[s].wait_recv()

    def go(self, s):
        if s > 0:
            self.arrive(s - 1)
        if s < self.steps:
            self.start(s)

    def drain(self):
        for way in (self.down, self.up):
            for copy in way:
                copy.wait_send()


def gather_kernel(
    nz, nx, ny, panels, pivots, a, inv, colg, ppg, rowg, invg,
    recv_c, recv_r, zbuf, xbuf, send_a, recv_a, send_b, recv_b, send_s, recv_s,
):
    rows, cols = 2 * nz, nx * ny
    half = panels // 2
    r, c = lax.axis_index("row"), lax.axis_index("col")
    z, core = r // 2, lax.rem(r, 2)
    x, y = c // ny, lax.rem(c, ny)

    barrier = pltpu.get_barrier_semaphore()

    def greet_col(d, carry):
        peer = lax.rem(c + d, cols)
        pl.semaphore_signal(barrier, inc=1, device_id={"col": peer}, device_id_type=MESH)
        return carry

    def greet_row(d, carry):
        peer = lax.rem(r + d, rows)
        pl.semaphore_signal(barrier, inc=1, device_id={"row": peer}, device_id_type=MESH)
        return carry

    lax.fori_loop(1, cols, greet_col, 0)
    lax.fori_loop(1, rows, greet_row, 0)
    pl.semaphore_wait(barrier, cols + rows - 2)

    sems = Sems(send_s, recv_s)

    def to_col(d):
        peer = lax.rem(c + d, cols)
        return pltpu.make_async_remote_copy(
            src_ref=a.at[:, peer], dst_ref=recv_c.at[c],
            send_sem=send_a.at[d], recv_sem=recv_a.at[d],
            device_id={"col": peer}, device_id_type=MESH,
        )

    def to_row(d):
        peer = lax.rem(r + d, rows)
        return pltpu.make_async_remote_copy(
            src_ref=a.at[:, pl.ds(2 * peer, 2)], dst_ref=recv_r.at[r],
            send_sem=send_b.at[d], recv_sem=recv_b.at[d],
            device_id={"row": peer}, device_id_type=MESH,
        )

    def loop(low, high, act):
        def body(d, carry):
            act(d)
            return carry
        lax.fori_loop(low, high, body, 0)

    loop(1, cols, lambda d: to_col(d).start())
    loop(1, rows, lambda d: to_row(d).start())

    y_right = {"col": x * ny + lax.rem(y + 1, ny)}
    y_left = {"col": x * ny + lax.rem(y + ny - 1, ny)}
    z_right = {"row": 2 * lax.rem(z + 1, nz) + core}
    z_left = {"row": 2 * lax.rem(z + nz - 1, nz) + core}
    partner = {"row": 2 * z + 1 - core}

    def ring_y(view):
        return Ring(sems, ny, y, view, y_right, y_left)

    def ring_z(view, first=None):
        return Ring(sems, nz, z, view, z_right, z_left, first)

    def spread_x(ref):
        copies = []
        for d in range(1, nx):
            peer = lax.rem(x + d, nx)
            copies.append(sems.copy(ref, ref, {"col": peer * ny + y}, sems.take()))
        return copies

    def start(copies):
        for copy in copies:
            copy.start()

    def to_partner(ref):
        return sems.copy(ref, ref, partner, sems.take())

    ring_inv = ring_z(lambda i: invg.at[i, core], inv)
    ring_inv.start(0)
    invg[z, core] = inv[...]
    recv_c[c] = a[:, c]
    recv_r[r] = a[:, pl.ds(2 * r, 2)]

    loop(1, cols, lambda d: to_col(d).wait_recv())
    for h in range(half):
        theirs = recv_c[pivots[(1 - core) * half + h]]
        for b in range(2):
            xbuf[b, h] = theirs[b]
    for m in range(panels):
        piece = recv_c[pivots[m]]
        for b in range(2):
            colg[b, x, y, m] = piece[b]
    for h in range(half):
        mine = recv_c[pivots[core * half + h]]
        for b in range(2):
            zbuf[z, 2 * core + b, h] = mine[b]

    swap = sems.copy(xbuf, zbuf.at[z, pl.ds(2 * core, 2)], partner, sems.take())
    swap.start()
    col0_x = spread_x(colg.at[0, x, y])
    start(col0_x)
    col1 = ring_y(lambda i: colg.at[1, x, i])
    col1.start(0)
    swap.wait_recv()
    ppz = ring_z(lambda i: zbuf.at[i])
    ppz.start(0)
    for copy in col0_x:
        copy.wait_recv()
    col0 = ring_y(lambda i: colg.at[0, :, i])
    col0.start(0)

    for s in range(1, max(nz // 2, ny // 2)):
        if s < nz // 2:
            ppz.go(s)
        if s < ny // 2:
            col1.go(s)
            if s > 1:
                col0.go(s - 1)
        if s < nz // 2:
            ring_inv.go(s)

    ppz.arrive(nz // 2 - 1)
    for h in range(half):
        m = core * half + h
        for j in range(panels - 1):
            k = j + (j >= m).astype(jnp.int32)
            p = pivots[k]
            ppg[m, x, y, j] = zbuf[p // 4, lax.rem(p, 4), h]
    m0, m1 = core * half, core * half + 1
    pp0_x = spread_x(ppg.at[m0, x, y])
    start(pp0_x)
    pp1 = ring_y(lambda i: ppg.at[m1, x, i])
    pp1.start(0)
    col1.arrive(ny // 2 - 1)
    col1_x = spread_x(colg.at[1, x])
    start(col1_x)
    col0.go(ny // 2 - 1)
    ring_inv.arrive(nz // 2 - 1)
    inv_swap = to_partner(invg.at[:, core])
    inv_swap.start()

    loop(1, rows, lambda d: to_row(d).wait_recv())
    for k in range(panels):
        p = pivots[k]
        rowg[z, core, k] = recv_r[p // 2, lax.rem(p, 2)]
    ring_row = ring_z(lambda i: rowg.at[i, core])
    ring_row.start(0)

    pp0 = ring_y(lambda i: ppg.at[m0, :, i])
    forwards = []

    def forward(ref):
        copy = to_partner(ref)
        copy.start()
        forwards.append(copy)

    for copy in pp0_x:
        copy.wait_recv()
    pp0.start(0)
    forward(ppg.at[m0, :, y])
    for s in range(1, max(nz // 2, ny // 2)):
        if s < ny // 2:
            pp1.go(s)
            if s > 1:
                pp0.go(s - 1)
                forward(ppg.at[m0, :, lax.rem(y - s + 1 + ny, ny)])
                forward(ppg.at[m0, :, lax.rem(y + s - 1, ny)])
        if s < nz // 2:
            ring_row.go(s)
    pp1.arrive(ny // 2 - 1)
    pp1_x = spread_x(ppg.at[m1, x])
    start(pp1_x)
    forward(ppg.at[m1, x])
    last = ny // 2 - 1
    if last > 0:
        pp0.go(last)
        forward(ppg.at[m0, :, lax.rem(y - last + ny, ny)])
        forward(ppg.at[m0, :, lax.rem(y + last, ny)])
    ring_row.arrive(nz // 2 - 1)
    row_swap = to_partner(rowg.at[:, core])
    row_swap.start()
    pp0.arrive(last)
    forward(ppg.at[m0, :, lax.rem(y + ny // 2, ny)])
    for d, copy in enumerate(pp1_x):
        copy.wait_recv()
        forward(ppg.at[m1, lax.rem(x - d - 1 + nx, nx)])
    col0.arrive(last)
    for copy in col1_x:
        copy.wait_recv()
    inv_swap.wait_recv()
    row_swap.wait_recv()
    for copy in forwards:
        copy.wait_recv()

    for ring in (ring_inv, ppz, col0, col1, pp0, pp1, ring_row):
        ring.drain()
    for copy in [swap, inv_swap, row_swap] + col0_x + col1_x + pp0_x + pp1_x + forwards:
        copy.wait_send()
    loop(1, cols, lambda d: to_col(d).wait_send())
    loop(1, rows, lambda d: to_row(d).wait_send())


def halves(value):
    high = value.astype(BF16)
    return high, (value - high.astype(F32)).astype(BF16)


def product(left, right):
    (lh, ll), (rh, rl) = left, right
    dot = functools.partial(jnp.dot, preferred_element_type=F32)
    return dot(lh, rh) + (dot(lh, rl) + dot(ll, rh))


def local_kernel(panels, width, place, pivots, row_mask, col_mask, a, colg, ppg, rowg, invg, out, work, xh, xl, keep):
    own = panels
    my_col = place[1]
    my_rows = [place[0] * 2 + b for b in range(2)]
    square = (width, width)

    for b in range(2):
        work[b, own] = a[b].reshape(square)
        for m in range(panels):
            work[b, m] = colg[b, :, :, m].reshape(square)
    for k in range(panels):
        work[2 + k, own] = rowg[:, :, k].reshape(square)
        for m in range(panels):
            if m != k:
                work[2 + k, m] = ppg[m, :, :, k - (k > m)].reshape(square)

    def done(block, step):
        hit = block == pivots[0]
        for k in range(1, step + 1):
            hit = hit | (block == pivots[k])
        return hit

    for step in range(panels):
        inverse = halves(invg[:, :, step].reshape(square))
        factors = [
            jnp.where(done(i, step), 0.0, row_mask[step, i].astype(F32)) for i in my_rows
        ] + [row_mask[step, pivots[k]].astype(F32) for k in range(step + 1, panels)]
        places = [0, 1] + [2 + k for k in range(step + 1, panels)]
        for n, (i, factor) in enumerate(zip(places, factors)):
            high, low = halves(work[i, step] * factor)
            xh[pl.ds(n * width, width), :] = high
            xl[pl.ds(n * width, width), :] = low
        my_factor = jnp.where(done(my_col, step), 0.0, col_mask[step, my_col].astype(F32))

        def column(j, carry):
            solved = product(inverse, halves(work[2 + step, j]))
            mine = j == own
            factor = jnp.where(
                mine, my_factor, col_mask[step, pivots[jnp.minimum(j, panels - 1)]].astype(F32)
            )

            @pl.when(mine)
            def _():
                keep[step] = solved

            right = halves(solved * factor)
            for n, i in enumerate(places):
                span = pl.ds(n * width, width)
                work[i, j] -= product((xh[span, :], xl[span, :]), right)
            return carry

        lax.fori_loop(step + 1, panels + 1, column, 0)

    for b in range(2):
        out[pl.ds(b * width, width), :] = work[b, own]
        for k in range(panels):
            mine = my_rows[b] == pivots[k]

            if k == 0:
                @pl.when(mine)
                def _():
                    out[pl.ds(b * width, width), :] = keep[0]
            else:
                gone = done(my_col, k - 1)

                @pl.when(mine & gone)
                def _():
                    out[pl.ds(b * width, width), :] = work[2 + k, own]

                @pl.when(mine & jnp.logical_not(gone))
                def _():
                    out[pl.ds(b * width, width), :] = keep[k]


def on_device(nz, nx, ny, matrix, inverses, pivots, row_mask, col_mask):
    panels, _, width = inverses.shape
    rows, cols = 2 * nz, nx * ny
    part = width // cols
    blocks = matrix.reshape(2, cols, part, width)
    slices = inverses.reshape(panels, 2, part, width)
    vmem = pl.BlockSpec(memory_space=pltpu.VMEM)
    smem = pl.BlockSpec(memory_space=pltpu.SMEM)
    half = panels // 2
    count = 256
    gathered = pl.pallas_call(
        functools.partial(gather_kernel, nz, nx, ny, panels),
        out_shape=(
            jax.ShapeDtypeStruct((2, nx, ny, panels, part, width), F32),
            jax.ShapeDtypeStruct((panels, nx, ny, panels - 1, part, width), F32),
            jax.ShapeDtypeStruct((nz, 2, panels, 2, part, width), F32),
            jax.ShapeDtypeStruct((nz, 2, panels, 2, part, width), F32),
        ),
        in_specs=[smem, vmem, vmem],
        out_specs=(vmem,) * 4,
        scratch_shapes=[
            pltpu.VMEM((cols, 2, part, width), F32),
            pltpu.VMEM((rows, 2, 2, part, width), F32),
            pltpu.VMEM((nz, 4, half, part, width), F32),
            pltpu.VMEM((2, half, part, width), F32),
            pltpu.SemaphoreType.DMA((cols,)),
            pltpu.SemaphoreType.DMA((cols,)),
            pltpu.SemaphoreType.DMA((rows,)),
            pltpu.SemaphoreType.DMA((rows,)),
            pltpu.SemaphoreType.DMA((count,)),
            pltpu.SemaphoreType.DMA((count,)),
        ],
        compiler_params=pltpu.CompilerParams(collective_id=0, has_side_effects=True),
        name="gather",
    )(pivots, blocks, slices)
    place = jnp.stack([lax.axis_index("row"), lax.axis_index("col")]).astype(jnp.int32)
    return pl.pallas_call(
        functools.partial(local_kernel, panels, width),
        out_shape=jax.ShapeDtypeStruct((2 * width, width), F32),
        in_specs=[smem] * 4 + [vmem] * 5,
        out_specs=vmem,
        scratch_shapes=[
            pltpu.VMEM((2 + panels, 1 + panels, width, width), F32),
            pltpu.VMEM(((1 + panels) * width, width), BF16),
            pltpu.VMEM(((1 + panels) * width, width), BF16),
            pltpu.VMEM((panels, width, width), F32),
        ],
        name="eliminate",
    )(place, pivots, row_mask, col_mask, blocks, *gathered)


def solution(mesh):
    rows, cols = mesh.shape["row"], mesh.shape["col"]
    nx = 4 if cols == 32 else 2
    in_specs = (P("row", "col"), P(None, "row", None), P(), P(), P())
    return jax.shard_map(
        functools.partial(on_device, rows // 2, nx, cols // nx),
        mesh=mesh, in_specs=in_specs, out_specs=P("row", "col"), check_vma=False,
    )
```

time: 1190 us -> 101 us (0.08)
  waiting for transfers between devices: 1120 us -> 0 us
  Pallas kernels: 0 us -> 99.9 us
  between operations: 33.3 us -> 0.01 us
  matrix products: 14.7 us -> 0 us
  other arithmetic: 12.7 us -> 0.59 us
    psum x8 -> x0, waiting for transfers between devices: 1070 us -> none  [from_root(): return lax.psum(block, axis)]
    pallas_call x0 -> x2, Pallas kernels: none -> 99.9 us  [the longest x1 85 us: on_device(): pl.pallas_call(functools.partial(gather_kernel, nz, nx, ny, panels), out_...]
    all_gather x1 -> x0, waiting for transfers between devices: 44.3 us -> none  [on_device(): full_inverse = lax.all_gather(inverses, 'row', axis=1, tiled=True)]
    dot_general x8 -> x0, matrix products: 14.7 us -> none  [the longest x4 9.16 us: on_device(): jnp.dot(left_part, right_part, precision=highest, preferred_element_type=...]
  transfers between devices with their start and end apart: 9 -> 0, of which waited for: 9 -> 0; matrix products, arithmetic and copies ran while one was open for 1% -> 0% of each run, Pallas kernels for 0% -> 0%
where the time goes in v1:
time: 101 us; the launch traced here: 100 us
  Pallas kernels  99.9 us (99%)
    pallas_call x1, Pallas kernels, on_device(): pl.pallas_call(functools.partial(gather_kernel, nz, nx, ny, panels), out_...  85 us
    pallas_call x1, Pallas kernels, on_device(): pl.pallas_call(functools.partial(local_kernel, panels, width), out_shape=...  14.9 us

profile of v1, /device:TPU:1, one launch (start us, length us, event | category | flops | bytes accessed | tf_op | source)
XLA Modules:
  0.0 100.5 jit_solution(9727115880499632746)
XLA Ops:
  0.0 0.6 pad_add_fusion.place
  0.6 85.0 %gather.1 = (f32[2,4,8,4,8,256]{5,4,3,2,1,0:T(8,128)}, f32[4,4,8,3,8,256]{5,4,3,2,1,0:T(8,128)}, f32[8,2,4,2,8,256]{5,4,3,2,1,0:T(8,128)}, f32[8,2,4,2,8,256]{5,4,3,2,1,0:T(8,128)}) custom-call(s32[4]{0:T(128)} %pivots.3, f32[2,32,8,256]{3,2,1,0:T(8,128)} %bitcast.4, f32[4,2,8,256]{3,2,1,0:T(8,128)} %bitcast.6), custom_call_target="tpu_custom_call" | custom-call | tf_op jit(solution)/shard_map/gather/pallas_call | solution.py:369
  85.6 14.9 %eliminate.1 = f32[512,256]{1,0:T(8,128)} custom-call(s32[2]{0:T(128)} %pad_add_fusion.place, s32[4]{0:T(128)} %pivots.3, s32[4,32]{1,0:T(4,128)} %row_mask.1, s32[4,32]{1,0:T(4,128)} %col_mask.1, f32[2,32,8,256]{3,2,1,0:T(8,128)} %bitcast.5, f32[2,4,8,4,8,256]{5,4,3,2,1,0:T(8,128)} %get-tuple-element.9.colg, ...), custom_call_target="tpu_custom_call" | custom-call | tf_op jit(solution)/shard_map/eliminate/pallas_call | solution.py:395

commit v2 on v1

--- a/solution.py
+++ b/solution.py
@@ -67,7 +67,7 @@
                 copy.wait_send()
 
 
-def gather_kernel(
+def gather(
     nz, nx, ny, panels, pivots, a, inv, colg, ppg, rowg, invg,
     recv_c, recv_r, zbuf, xbuf, send_a, recv_a, send_b, recv_b, send_s, recv_s,
 ):
@@ -282,21 +282,18 @@
     return dot(lh, rh) + (dot(lh, rl) + dot(ll, rh))
 
 
-def local_kernel(panels, width, place, pivots, row_mask, col_mask, a, colg, ppg, rowg, invg, out, work, xh, xl, keep):
-    own = panels
-    my_col = place[1]
-    my_rows = [place[0] * 2 + b for b in range(2)]
+def eliminate(panels, width, pivots, row_mask, col_mask, a, colg, ppg, rowg, invg, out, xh, xl, keep):
+    my_col = lax.axis_index("col")
+    my_rows = [lax.axis_index("row") * 2 + b for b in range(2)]
     square = (width, width)
 
-    for b in range(2):
-        work[b, own] = a[b].reshape(square)
-        for m in range(panels):
-            work[b, m] = colg[b, :, :, m].reshape(square)
-    for k in range(panels):
-        work[2 + k, own] = rowg[:, :, k].reshape(square)
-        for m in range(panels):
-            if m != k:
-                work[2 + k, m] = ppg[m, :, :, k - (k > m)].reshape(square)
+    def whole(ref, *index):
+        return ref[index].reshape(square)
+
+    def left_of(i, step):
+        if i < 2:
+            return whole(colg, i, slice(None), slice(None), step)
+        return whole(ppg, step, slice(None), slice(None), i - 2 - (i - 2 > step))
 
     def done(block, step):
         hit = block == pivots[0]
@@ -305,55 +302,53 @@
         return hit
 
     for step in range(panels):
-        inverse = halves(invg[:, :, step].reshape(square))
-        factors = [
-            jnp.where(done(i, step), 0.0, row_mask[step, i].astype(F32)) for i in my_rows
-        ] + [row_mask[step, pivots[k]].astype(F32) for k in range(step + 1, panels)]
-        places = [0, 1] + [2 + k for k in range(step + 1, panels)]
+        inverse = halves(whole(invg, slice(None), slice(None), step))
+        later = range(step + 1, panels)
+        factors = [jnp.where(done(i, step), 0.0, row_mask[step, i].astype(F32)) for i in my_rows]
+        factors += [row_mask[step, pivots[k]].astype(F32) for k in later]
+        places = [0, 1] + [2 + k for k in later]
         for n, (i, factor) in enumerate(zip(places, factors)):
-            high, low = halves(work[i, step] * factor)
-            xh[pl.ds(n * width, width), :] = high
-            xl[pl.ds(n * width, width), :] = low
-        my_factor = jnp.where(done(my_col, step), 0.0, col_mask[step, my_col].astype(F32))
-
-        def column(j, carry):
-            solved = product(inverse, halves(work[2 + step, j]))
-            mine = j == own
-            factor = jnp.where(
-                mine, my_factor, col_mask[step, pivots[jnp.minimum(j, panels - 1)]].astype(F32)
-            )
-
-            @pl.when(mine)
-            def _():
-                keep[step] = solved
-
-            right = halves(solved * factor)
+            high, low = halves(left_of(i, step) * factor)
+            xh[n] = high
+            xl[n] = low
+        for j in later:
+            solved = product(inverse, halves(left_of(2 + step, j)))
+            right = halves(solved * col_mask[step, pivots[j]].astype(F32))
             for n, i in enumerate(places):
-                span = pl.ds(n * width, width)
-                work[i, j] -= product((xh[span, :], xl[span, :]), right)
-            return carry
-
-        lax.fori_loop(step + 1, panels + 1, column, 0)
+                if i - 2 == j:
+                    continue
+                change = product((xh[n], xl[n]), right)
+                if i < 2:
+                    shape = colg.shape[1:3] + colg.shape[4:]
+                    colg[i, :, :, j] -= change.reshape(shape)
+                else:
+                    shape = ppg.shape[1:3] + ppg.shape[4:]
+                    ppg[j, :, :, i - 2 - (i - 2 > j)] -= change.reshape(shape)
+        solved = product(inverse, halves(whole(rowg, slice(None), slice(None), step)))
+        keep[step] = solved
+        factor = jnp.where(done(my_col, step), 0.0, col_mask[step, my_col].astype(F32))
+        right = halves(solved * factor)
+        for n, i in enumerate(places):
+            change = product((xh[n], xl[n]), right)
+            if i < 2:
+                span = pl.ds(i * width, width)
+                before = whole(a, i) if step == 0 else out[span, :]
+                out[span, :] = before - change
+            else:
+                shape = rowg.shape[:2] + rowg.shape[3:]
+                rowg[:, :, i - 2] -= change.reshape(shape)
 
     for b in range(2):
-        out[pl.ds(b * width, width), :] = work[b, own]
+        span = pl.ds(b * width, width)
+        value = out[span, :]
         for k in range(panels):
             mine = my_rows[b] == pivots[k]
-
             if k == 0:
-                @pl.when(mine)
-                def _():
-                    out[pl.ds(b * width, width), :] = keep[0]
+                pivot_row = keep[k]
             else:
-                gone = done(my_col, k - 1)
-
-                @pl.when(mine & gone)
-                def _():
-                    out[pl.ds(b * width, width), :] = work[2 + k, own]
-
-                @pl.when(mine & jnp.logical_not(gone))
-                def _():
-                    out[pl.ds(b * width, width), :] = keep[k]
+                pivot_row = jnp.where(done(my_col, k - 1), whole(rowg, slice(None), slice(None), k), keep[k])
+            value = jnp.where(mine, pivot_row, value)
+        out[span, :] = value
 
 
 def on_device(nz, nx, ny, matrix, inverses, pivots, row_mask, col_mask):
@@ -366,17 +361,19 @@
     smem = pl.BlockSpec(memory_space=pltpu.SMEM)
     half = panels // 2
     count = 256
-    gathered = pl.pallas_call(
-        functools.partial(gather_kernel, nz, nx, ny, panels),
-        out_shape=(
-            jax.ShapeDtypeStruct((2, nx, ny, panels, part, width), F32),
-            jax.ShapeDtypeStruct((panels, nx, ny, panels - 1, part, width), F32),
-            jax.ShapeDtypeStruct((nz, 2, panels, 2, part, width), F32),
-            jax.ShapeDtypeStruct((nz, 2, panels, 2, part, width), F32),
-        ),
-        in_specs=[smem, vmem, vmem],
-        out_specs=(vmem,) * 4,
+    return pl.pallas_call(
+        functools.partial(kernel, nz, nx, ny, panels, width),
+        out_shape=jax.ShapeDtypeStruct((2 * width, width), F32),
+        in_specs=[smem, smem, smem, vmem, vmem],
+        out_specs=vmem,
         scratch_shapes=[
+            pltpu.VMEM((2, nx, ny, panels, part, width), F32),
+            pltpu.VMEM((panels, nx, ny, panels - 1, part, width), F32),
+            pltpu.VMEM((nz, 2, panels, 2, part, width), F32),
+            pltpu.VMEM((nz, 2, panels, 2, part, width), F32),
+            pltpu.VMEM((1 + panels, width, width), BF16),
+            pltpu.VMEM((1 + panels, width, width), BF16),
+            pltpu.VMEM((panels, width, width), F32),
             pltpu.VMEM((cols, 2, part, width), F32),
             pltpu.VMEM((rows, 2, 2, part, width), F32),
             pltpu.VMEM((nz, 4, half, part, width), F32),
@@ -389,22 +386,15 @@
             pltpu.SemaphoreType.DMA((count,)),
         ],
         compiler_params=pltpu.CompilerParams(collective_id=0, has_side_effects=True),
-        name="gather",
-    )(pivots, blocks, slices)
-    place = jnp.stack([lax.axis_index("row"), lax.axis_index("col")]).astype(jnp.int32)
-    return pl.pallas_call(
-        functools.partial(local_kernel, panels, width),
-        out_shape=jax.ShapeDtypeStruct((2 * width, width), F32),
-        in_specs=[smem] * 4 + [vmem] * 5,
-        out_specs=vmem,
-        scratch_shapes=[
-            pltpu.VMEM((2 + panels, 1 + panels, width, width), F32),
-            pltpu.VMEM(((1 + panels) * width, width), BF16),
-            pltpu.VMEM(((1 + panels) * width, width), BF16),
-            pltpu.VMEM((panels, width, width), F32),
-        ],
-        name="eliminate",
-    )(place, pivots, row_mask, col_mask, blocks, *gathered)
+    )(pivots, row_mask, col_mask, blocks, slices)
+
+
+def kernel(
+    nz, nx, ny, panels, width, pivots, row_mask, col_mask, a, inv, out,
+    colg, ppg, rowg, invg, xh, xl, keep, *scratch,
+):
+    gather(nz, nx, ny, panels, pivots, a, inv, colg, ppg, rowg, invg, *scratch)
+    eliminate(panels, width, pivots, row_mask, col_mask, a, colg, ppg, rowg, invg, out, xh, xl, keep)
 
 
 def solution(mesh):

time: 101 us -> 92 us (0.911)
  Pallas kernels: 99.9 us -> 90 us
  local copies, waits for them, and re-layouts: 0 us -> 1.87 us
    pallas_call x2 -> x1, Pallas kernels: 99.9 us -> 90 us  [on_device(): pl.pallas_call(functools.partial(kernel, nz, nx, ny, panels, width), out_...]
    unnamed x0 -> x1, local copies, waits for them, and re-layouts: none -> 1.87 us
where the time goes in v2:
time: 92 us; the launch traced here: 91.9 us
  Pallas kernels  90 us (98%)
  local copies, waits for them, and re-layouts  1.87 us (2%)
    pallas_call x1, Pallas kernels, on_device(): pl.pallas_call(functools.partial(kernel, nz, nx, ny, panels, width), out_...  90 us
    unnamed x1, local copies, waits for them, and re-layouts  1.87 us

profile of v2, /device:TPU:1, one launch (start us, length us, event | category | flops | bytes accessed | tf_op | source)
XLA Modules:
  0.0 91.9 jit_solution(6174664466407240725)
XLA Ops:
  0.0 90.0 %shard_map.55 = f32[512,256]{1,0:T(8,128)} custom-call(s32[4]{0:T(128)} %pivots.1, s32[4,32]{1,0:T(4,128)} %row_mask.1, s32[4,32]{1,0:T(4,128)} %col_mask.1, f32[2,32,8,256]{3,2,1,0:T(8,128)} %bitcast.2, f32[4,2,8,256]{3,2,1,0:T(8,128)} %bitcast.3), custom_call_target="tpu_custom_call" | custom-call | tf_op jit(solution)/shard_map/pallas_call | solution.py:364
  90.0 1.9 %copy.7 = f32[512,256]{1,0:T(8,128)} copy(f32[512,256]{1,0:T(8,128)} %shard_map.55) | data formatting | bytes 1048576

commit v3 on v2

v3 whole, which is shorter than its diff:
```python
import functools

import jax
import jax.numpy as jnp
from jax import lax
from jax.experimental import pallas as pl
from jax.experimental.pallas import tpu as pltpu
from jax.sharding import PartitionSpec as P

MESH = pl.DeviceIdType.MESH
F32 = jnp.float32
BF16 = jnp.bfloat16
CHUNKS = 1
TIMES = {
    "a2a": (10.0,), "rows": 24.0, "swap": 2.5, "z": 5.0, "inv": 8.0, "row": 8.0, "share": 3.0,
    "col": ((5.0, 4.5), (5.0, 1.2)), "pp": ((3.5, 6.0), (4.0, 0.6)),
}


class Sems:
    def __init__(self, send, recv):
        self.send, self.recv, self.used = send, recv, 0

    def take(self, count=1):
        first = self.used
        self.used += count
        return first

    def copy(self, src, dst, device, index):
        return pltpu.make_async_remote_copy(
            src_ref=src,
            dst_ref=dst,
            send_sem=self.send.at[index],
            recv_sem=self.recv.at[index],
            device_id=device,
            device_id_type=MESH,
        )


class Ring:
    def __init__(self, sems, n, me, views, right, left):
        self.n, self.me, self.steps = n, me, n // 2
        self.pieces = []
        for view in views:
            ways = []
            for s in range(self.steps):
                slot = lax.rem(me - s + n, n)
                ways.append([sems.copy(view(slot), view(slot), right, sems.take())])
                if s < n - 1 - self.steps:
                    slot = lax.rem(me + s, n)
                    ways[-1].append(sems.copy(view(slot), view(slot), left, sems.take()))
            self.pieces.append(ways)

    def run(self, delay, arrived=None):
        for s in range(self.steps + 1):
            for n, ways in enumerate(self.pieces):
                if s > 0:
                    yield 0.3 if n else delay
                    for copy in ways[s - 1]:
                        copy.wait_recv()
                if s < self.steps:
                    for copy in ways[s]:
                        copy.start()
            if s > 0 and arrived is not None:
                arrived(lax.rem(self.me - s + self.n, self.n))
                if s < self.n - self.steps:
                    arrived(lax.rem(self.me + s, self.n))

    def drain(self):
        for ways in self.pieces:
            for step in ways:
                for copy in step:
                    copy.wait_send()


class Hops:
    def __init__(self, sems, n, me, views, at):
        self.n, self.me, self.all = n, me, []
        self.first, self.second = [], []

        def copy(view, slot, to):
            slot = lax.rem(me + slot + n, n)
            made = sems.copy(view(slot), view(slot), at(lax.rem(me + to + n, n)), sems.take())
            self.all.append(made)
            return made

        for p, view in enumerate(views):
            if n < 6:
                self.first.append([copy(view, 0, d) for d in range(1, n)])
                self.second.append([])
            else:
                self.first.append([copy(view, 0, d) for d in (2, -2, 1, -1)])
                far = 2 if p % 2 == 0 else -2
                self.second.append([copy(view, -2, 1), copy(view, 2, -1), copy(view, -far, far)])

    def slot(self, d):
        return lax.rem(self.me + d + self.n, self.n)

    def run(self, delay, arrived=None):
        for copies in self.first:
            for copy in copies:
                copy.start()
        for n, copies in enumerate(self.first):
            yield 0.3 if n else delay
            for copy in copies[:2]:
                copy.wait_recv()
            for copy in self.second[n]:
                copy.start()
        for copies in self.first:
            for copy in copies[2:]:
                copy.wait_recv()
        near = [-d for d in range(1, self.n)] if self.n < 6 else [-1, 1, -2, 2]
        if arrived is not None:
            for d in near:
                arrived(self.slot(d))
        if self.n >= 6:
            for n, copies in enumerate(self.second):
                yield 0.3 if n else delay
                for copy in copies:
                    copy.wait_recv()
            if arrived is not None:
                for d in (-3, 3, 4):
                    arrived(self.slot(d))

    def drain(self):
        for copy in self.all:
            copy.wait_send()


def interleave(chains):
    queue = [(start, n, chain) for n, (start, chain) in enumerate(chains)]
    count = len(queue)
    while queue:
        now, n, chain = min(queue, key=lambda item: item[:2])
        queue.remove((now, n, chain))
        for event in chain:
            if isinstance(event, tuple):
                queue.append((now + event[0], count, event[1]))
                count += 1
            else:
                queue.append((now + event, n, chain))
                break


def gather(
    nz, nx, ny, panels, pivots, a, inv, colg, ppg, rowg, invg,
    recv_c, recv_r, zbuf, xbuf, send_a, recv_a, send_b, recv_b, send_s, recv_s,
):
    rows, cols = 2 * nz, nx * ny
    half = panels // 2
    r, c = lax.axis_index("row"), lax.axis_index("col")
    z, core = r // 2, lax.rem(r, 2)
    x, y = c // ny, lax.rem(c, ny)
    lanes = colg.shape[-1] // CHUNKS

    barrier = pltpu.get_barrier_semaphore()

    def loop(low, high, act):
        def body(d, carry):
            act(d)
            return carry
        lax.fori_loop(low, high, body, 0)

    def greet(axis, me, n):
        loop(1, n, lambda d: pl.semaphore_signal(
            barrier, inc=1, device_id={axis: lax.rem(me + d, n)}, device_id_type=MESH
        ))

    greet("col", c, cols)
    greet("row", r, rows)
    recv_c[c] = a[:, c]
    recv_r[r] = a[:, pl.ds(2 * r, 2)]
    invg[z, core] = inv[...]
    pl.semaphore_wait(barrier, cols + rows - 2)

    sems = Sems(send_s, recv_s)

    def span(part):
        return pl.ds(part * lanes, lanes)

    def to_col(part, d):
        peer = lax.rem(c + d, cols)
        return pltpu.make_async_remote_copy(
            src_ref=a.at[:, peer, :, span(part)], dst_ref=recv_c.at[c, :, :, span(part)],
            send_sem=send_a.at[part, d], recv_sem=recv_a.at[part, d],
            device_id={"col": peer}, device_id_type=MESH,
        )

    def to_row(d):
        peer = lax.rem(r + d, rows)
        return pltpu.make_async_remote_copy(
            src_ref=a.at[:, pl.ds(2 * peer, 2)], dst_ref=recv_r.at[r],
            send_sem=send_b.at[d], recv_sem=recv_b.at[d],
            device_id={"row": peer}, device_id_type=MESH,
        )

    for part in range(CHUNKS):
        loop(1, cols, lambda d: to_col(part, d).start())
    loop(1, rows, lambda d: to_row(d).start())

    y_right = {"col": x * ny + lax.rem(y + 1, ny)}
    y_left = {"col": x * ny + lax.rem(y + ny - 1, ny)}
    partner = {"row": 2 * z + 1 - core}
    rings, copies = [], []

    def ring_y(*views):
        rings.append(Ring(sems, ny, y, views, y_right, y_left))
        return rings[-1]

    def hops_y(*views):
        rings.append(Hops(sems, ny, y, views, lambda i: {"col": x * ny + i}))
        return rings[-1]

    def hops_z(*views):
        rings.append(Hops(sems, nz, z, views, lambda i: {"row": 2 * i + core}))
        return rings[-1]

    def send(src, dst, device):
        copy = sems.copy(src, dst, device, sems.take())
        copy.start()
        copies.append(copy)
        return copy

    def spread_x(ref):
        return [
            send(ref, ref, {"col": lax.rem(x + d, nx) * ny + y}) for d in range(1, nx)
        ]

    forwards = []

    def forward(ref):
        forwards.append(send(ref, ref, partner))

    def x_then_y(gather_y, view, first, step, arrived):
        copies = spread_x(view(x, y))
        yield first
        for copy in copies:
            copy.wait_recv()
        arrived(y)
        yield from gather_y(*[lambda i, k=k: view(k, i) for k in range(nx)]).run(step, arrived)

    def y_then_x(gather_y, view, first, spread, arrived):
        pending = []

        def have(i):
            pending.append((i, spread_x(view(x, i))))

        have(y)
        yield from gather_y(lambda i: view(x, i)).run(first, have)
        for i, copies in pending:
            yield spread
            for copy in copies:
                copy.wait_recv()
            arrived(i)

    def cross_chain(part):
        swap = send(
            xbuf.at[:, :, :, span(part)], zbuf.at[z, pl.ds(2 * core, 2), :, :, span(part)], partner
        )
        yield TIMES["swap"]
        swap.wait_recv()
        yield from hops_z(
            *[lambda i, k=k: zbuf.at[i, pl.ds(2 * k, 2), :, :, span(part)] for k in range(2)]
        ).run(TIMES["z"])
        for h in range(half):
            m = core * half + h
            for j in range(panels - 1):
                p = pivots[j + (j >= m).astype(jnp.int32)]
                ppg[m, x, y, j, :, span(part)] = zbuf[p // 4, lax.rem(p, 4), h, :, span(part)]
        for h, order in ((0, x_then_y), (1, y_then_x)):
            m = core * half + h

            def view(i, j, m=m):
                return ppg.at[m, i, j, :, :, span(part)]

            def arrived(i, view=view):
                forward(view(slice(None), i))

            yield (0, order(hops_y, view, *TIMES["pp"][h], arrived))

    def column_chain(part):
        loop(1, cols, lambda d: to_col(part, d).wait_recv())
        for h in range(half):
            theirs = recv_c[pivots[(1 - core) * half + h], :, :, span(part)]
            mine = recv_c[pivots[core * half + h], :, :, span(part)]
            for b in range(2):
                xbuf[b, h, :, span(part)] = theirs[b]
                zbuf[z, 2 * core + b, h, :, span(part)] = mine[b]
        for m in range(panels):
            piece = recv_c[pivots[m], :, :, span(part)]
            for b in range(2):
                colg[b, x, y, m, :, span(part)] = piece[b]
        yield (0, cross_chain(part))
        for b, order in ((0, x_then_y), (1, y_then_x)):

            def view(i, j, b=b):
                return colg.at[b, i, j, :, :, span(part)]

            yield (0, order((ring_y, hops_y)[b], view, *TIMES["col"][b], lambda i: None))

    def partner_swap(ref):
        copy = send(ref, ref, partner)
        yield TIMES["share"]
        copy.wait_recv()

    def inverse_chain():
        yield 0
        yield from hops_z(lambda i: invg.at[i, core]).run(TIMES["inv"])
        yield from partner_swap(invg.at[:, core])

    def row_chain():
        loop(1, rows, lambda d: to_row(d).wait_recv())
        for k in range(panels):
            p = pivots[k]
            rowg[z, core, k] = recv_r[p // 2, lax.rem(p, 2)]
        yield from hops_z(lambda i: rowg.at[i, core]).run(TIMES["row"])
        yield from partner_swap(rowg.at[:, core])

    interleave(
        [(TIMES["a2a"][part], column_chain(part)) for part in range(CHUNKS)]
        + [(TIMES["rows"], row_chain()), (23.0, inverse_chain())]
    )
    for copy in forwards:
        copy.wait_recv()
    for ring in rings:
        ring.drain()
    for copy in copies:
        copy.wait_send()
    for part in range(CHUNKS):
        loop(1, cols, lambda d: to_col(part, d).wait_send())
    loop(1, rows, lambda d: to_row(d).wait_send())


def halves(value):
    high = value.astype(BF16)
    return high, (value - high.astype(F32)).astype(BF16)


def product(left, right):
    (lh, ll), (rh, rl) = left, right
    dot = functools.partial(jnp.dot, preferred_element_type=F32)
    return dot(lh, rh) + (dot(lh, rl) + dot(ll, rh))


def eliminate(panels, width, pivots, row_mask, col_mask, a, colg, ppg, rowg, invg, out, xh, xl, keep):
    my_col = lax.axis_index("col")
    my_rows = [lax.axis_index("row") * 2 + b for b in range(2)]
    square = (width, width)

    def whole(ref, *index):
        return ref[index].reshape(square)

    def left_of(i, step):
        if i < 2:
            return whole(colg, i, slice(None), slice(None), step)
        return whole(ppg, step, slice(None), slice(None), i - 2 - (i - 2 > step))

    def done(block, step):
        hit = block == pivots[0]
        for k in range(1, step + 1):
            hit = hit | (block == pivots[k])
        return hit

    for step in range(panels):
        inverse = halves(whole(invg, slice(None), slice(None), step))
        later = range(step + 1, panels)
        factors = [jnp.where(done(i, step), 0.0, row_mask[step, i].astype(F32)) for i in my_rows]
        factors += [row_mask[step, pivots[k]].astype(F32) for k in later]
        places = [0, 1] + [2 + k for k in later]
        for n, (i, factor) in enumerate(zip(places, factors)):
            high, low = halves(left_of(i, step) * factor)
            xh[n] = high
            xl[n] = low
        for j in later:
            solved = product(inverse, halves(left_of(2 + step, j)))
            right = halves(solved * col_mask[step, pivots[j]].astype(F32))
            for n, i in enumerate(places):
                if i - 2 == j:
                    continue
                change = product((xh[n], xl[n]), right)
                if i < 2:
                    shape = colg.shape[1:3] + colg.shape[4:]
                    colg[i, :, :, j] -= change.reshape(shape)
                else:
                    shape = ppg.shape[1:3] + ppg.shape[4:]
                    ppg[j, :, :, i - 2 - (i - 2 > j)] -= change.reshape(shape)
        solved = product(inverse, halves(whole(rowg, slice(None), slice(None), step)))
        keep[step] = solved
        factor = jnp.where(done(my_col, step), 0.0, col_mask[step, my_col].astype(F32))
        right = halves(solved * factor)
        for n, i in enumerate(places):
            change = product((xh[n], xl[n]), right)
            if i < 2:
                span = pl.ds(i * width, width)
                before = whole(a, i) if step == 0 else out[span, :]
                out[span, :] = before - change
            else:
                shape = rowg.shape[:2] + rowg.shape[3:]
                rowg[:, :, i - 2] -= change.reshape(shape)

    for b in range(2):
        span = pl.ds(b * width, width)
        value = out[span, :]
        for k in range(panels):
            mine = my_rows[b] == pivots[k]
            if k == 0:
                pivot_row = keep[k]
            else:
                pivot_row = jnp.where(done(my_col, k - 1), whole(rowg, slice(None), slice(None), k), keep[k])
            value = jnp.where(mine, pivot_row, value)
        out[span, :] = value


def on_device(nz, nx, ny, matrix, inverses, pivots, row_mask, col_mask):
    panels, _, width = inverses.shape
    rows, cols = 2 * nz, nx * ny
    part = width // cols
    blocks = matrix.reshape(2, cols, part, width)
    slices = inverses.reshape(panels, 2, part, width)
    vmem = pl.BlockSpec(memory_space=pltpu.VMEM)
    smem = pl.BlockSpec(memory_space=pltpu.SMEM)
    half = panels // 2
    count = 320
    return pl.pallas_call(
        functools.partial(kernel, nz, nx, ny, panels, width),
        out_shape=jax.ShapeDtypeStruct((2 * width, width), F32),
        in_specs=[smem, smem, smem, vmem, vmem],
        out_specs=vmem,
        scratch_shapes=[
            pltpu.VMEM((2, nx, ny, panels, part, width), F32),
            pltpu.VMEM((panels, nx, ny, panels - 1, part, width), F32),
            pltpu.VMEM((nz, 2, panels, 2, part, width), F32),
            pltpu.VMEM((nz, 2, panels, 2, part, width), F32),
            pltpu.VMEM((1 + panels, width, width), BF16),
            pltpu.VMEM((1 + panels, width, width), BF16),
            pltpu.VMEM((panels, width, width), F32),
            pltpu.VMEM((cols, 2, part, width), F32),
            pltpu.VMEM((rows, 2, 2, part, width), F32),
            pltpu.VMEM((nz, 4, half, part, width), F32),
            pltpu.VMEM((2, half, part, width), F32),
            pltpu.SemaphoreType.DMA((CHUNKS, cols)),
            pltpu.SemaphoreType.DMA((CHUNKS, cols)),
            pltpu.SemaphoreType.DMA((rows,)),
            pltpu.SemaphoreType.DMA((rows,)),
            pltpu.SemaphoreType.DMA((count,)),
            pltpu.SemaphoreType.DMA((count,)),
        ],
        compiler_params=pltpu.CompilerParams(collective_id=0, has_side_effects=True),
    )(pivots, row_mask, col_mask, blocks, slices)


def kernel(
    nz, nx, ny, panels, width, pivots, row_mask, col_mask, a, inv, out,
    colg, ppg, rowg, invg, xh, xl, keep, *scratch,
):
    gather(nz, nx, ny, panels, pivots, a, inv, colg, ppg, rowg, invg, *scratch)
    eliminate(panels, width, pivots, row_mask, col_mask, a, colg, ppg, rowg, invg, out, xh, xl, keep)


def solution(mesh):
    rows, cols = mesh.shape["row"], mesh.shape["col"]
    nx = 4 if cols == 32 else 2
    in_specs = (P("row", "col"), P(None, "row", None), P(), P(), P())
    return jax.shard_map(
        functools.partial(on_device, rows // 2, nx, cols // nx),
        mesh=mesh, in_specs=in_specs, out_specs=P("row", "col"), check_vma=False,
    )
```

time: 92 us -> 85.5 us (0.929)
  Pallas kernels: 90 us -> 83.4 us
    pallas_call x1, Pallas kernels: 90 us -> 83.4 us  [on_device(): pl.pallas_call(functools.partial(kernel, nz, nx, ny, panels, width), out_...]
where the time goes in v3:
time: 85.5 us; the launch traced here: 85.3 us
  Pallas kernels  83.4 us (98%)
  local copies, waits for them, and re-layouts  1.87 us (2%)
    pallas_call x1, Pallas kernels, on_device(): pl.pallas_call(functools.partial(kernel, nz, nx, ny, panels, width), out_...  83.4 us
    unnamed x1, local copies, waits for them, and re-layouts  1.87 us

profile of v3, /device:TPU:1, one launch (start us, length us, event | category | flops | bytes accessed | tf_op | source)
XLA Modules:
  0.0 85.3 jit_solution(2428789315846765742)
XLA Ops:
  0.0 83.4 %shard_map.55 = f32[512,256]{1,0:T(8,128)} custom-call(s32[4]{0:T(128)} %pivots.1, s32[4,32]{1,0:T(4,128)} %row_mask.1, s32[4,32]{1,0:T(4,128)} %col_mask.1, f32[2,32,8,256]{3,2,1,0:T(8,128)} %bitcast.2, f32[4,2,8,256]{3,2,1,0:T(8,128)} %bitcast.3), custom_call_target="tpu_custom_call" | custom-call | tf_op jit(solution)/shard_map/pallas_call | solution.py:424
  83.4 1.9 %copy.7 = f32[512,256]{1,0:T(8,128)} copy(f32[512,256]{1,0:T(8,128)} %shard_map.55) | data formatting | bytes 1048576

commit v4 on v3

--- a/solution.py
+++ b/solution.py
@@ -11,6 +11,7 @@
 F32 = jnp.float32
 BF16 = jnp.bfloat16
 CHUNKS = 1
+SPLIT = 1
 TIMES = {
     "a2a": (10.0,), "rows": 24.0, "swap": 2.5, "z": 5.0, "inv": 8.0, "row": 8.0, "share": 3.0,
     "col": ((5.0, 4.5), (5.0, 1.2)), "pp": ((3.5, 6.0), (4.0, 0.6)),
@@ -143,7 +144,7 @@
 
 
 def gather(
-    nz, nx, ny, panels, pivots, a, inv, colg, ppg, rowg, invg,
+    nz, nx, ny, panels, pivots, a_in, a, load_sem, inv, colg, ppg, rowg, invg,
     recv_c, recv_r, zbuf, xbuf, send_a, recv_a, send_b, recv_b, send_s, recv_s,
 ):
     rows, cols = 2 * nz, nx * ny
@@ -166,8 +167,11 @@
             barrier, inc=1, device_id={axis: lax.rem(me + d, n)}, device_id_type=MESH
         ))
 
+    load = pltpu.make_async_copy(a_in, a, load_sem)
+    load.start()
     greet("col", c, cols)
     greet("row", r, rows)
+    load.wait()
     recv_c[c] = a[:, c]
     recv_r[r] = a[:, pl.ds(2 * r, 2)]
     invg[z, core] = inv[...]
@@ -266,12 +270,15 @@
             m = core * half + h
             for j in range(panels - 1):
                 p = pivots[j + (j >= m).astype(jnp.int32)]
-                ppg[m, x, y, j, :, span(part)] = zbuf[p // 4, lax.rem(p, 4), h, :, span(part)]
+                ppg[core, x, y, h * (panels - 1) + j, :, span(part)] = zbuf[
+                    p // 4, lax.rem(p, 4), h, :, span(part)
+                ]
+        whole = half * (panels - 1)
         for h, order in ((0, x_then_y), (1, y_then_x)):
-            m = core * half + h
-
-            def view(i, j, m=m):
-                return ppg.at[m, i, j, :, :, span(part)]
+            some = pl.ds(0, SPLIT) if h == 0 else pl.ds(SPLIT, whole - SPLIT)
+
+            def view(i, j, some=some):
+                return ppg.at[core, i, j, some, :, span(part)]
 
             def arrived(i, view=view):
                 forward(view(slice(None), i))
@@ -350,10 +357,14 @@
     def whole(ref, *index):
         return ref[index].reshape(square)
 
+    def crossing(k, m):
+        half = panels // 2
+        return m // half, slice(None), slice(None), m % half * (panels - 1) + k - (k > m)
+
     def left_of(i, step):
         if i < 2:
             return whole(colg, i, slice(None), slice(None), step)
-        return whole(ppg, step, slice(None), slice(None), i - 2 - (i - 2 > step))
+        return whole(ppg, *crossing(i - 2, step))
 
     def done(block, step):
         hit = block == pivots[0]
@@ -383,7 +394,7 @@
                     colg[i, :, :, j] -= change.reshape(shape)
                 else:
                     shape = ppg.shape[1:3] + ppg.shape[4:]
-                    ppg[j, :, :, i - 2 - (i - 2 > j)] -= change.reshape(shape)
+                    ppg[crossing(i - 2, j)] -= change.reshape(shape)
         solved = product(inverse, halves(whole(rowg, slice(None), slice(None), step)))
         keep[step] = solved
         factor = jnp.where(done(my_col, step), 0.0, col_mask[step, my_col].astype(F32))
@@ -424,11 +435,13 @@
     return pl.pallas_call(
         functools.partial(kernel, nz, nx, ny, panels, width),
         out_shape=jax.ShapeDtypeStruct((2 * width, width), F32),
-        in_specs=[smem, smem, smem, vmem, vmem],
+        in_specs=[smem, smem, smem, pl.BlockSpec(memory_space=pl.ANY), vmem],
         out_specs=vmem,
         scratch_shapes=[
+            pltpu.VMEM((2, cols, part, width), F32),
+            pltpu.SemaphoreType.DMA,
             pltpu.VMEM((2, nx, ny, panels, part, width), F32),
-            pltpu.VMEM((panels, nx, ny, panels - 1, part, width), F32),
+            pltpu.VMEM((2, nx, ny, half * (panels - 1), part, width), F32),
             pltpu.VMEM((nz, 2, panels, 2, part, width), F32),
             pltpu.VMEM((nz, 2, panels, 2, part, width), F32),
             pltpu.VMEM((1 + panels, width, width), BF16),
@@ -450,10 +463,10 @@
 
 
 def kernel(
-    nz, nx, ny, panels, width, pivots, row_mask, col_mask, a, inv, out,
-    colg, ppg, rowg, invg, xh, xl, keep, *scratch,
+    nz, nx, ny, panels, width, pivots, row_mask, col_mask, a_in, inv, out,
+    a, load_sem, colg, ppg, rowg, invg, xh, xl, keep, *scratch,
 ):
-    gather(nz, nx, ny, panels, pivots, a, inv, colg, ppg, rowg, invg, *scratch)
+    gather(nz, nx, ny, panels, pivots, a_in, a, load_sem, inv, colg, ppg, rowg, invg, *scratch)
     eliminate(panels, width, pivots, row_mask, col_mask, a, colg, ppg, rowg, invg, out, xh, xl, keep)
 
 

time: 85.5 us -> 83.2 us (0.973)
  Pallas kernels: 83.4 us -> 81.1 us
    pallas_call x1, Pallas kernels: 83.4 us -> 81.1 us  [on_device(): pl.pallas_call(functools.partial(kernel, nz, nx, ny, panels, width), out_...]
where the time goes in v4:
time: 83.2 us; the launch traced here: 83 us
  Pallas kernels  81.1 us (97%)
  local copies, waits for them, and re-layouts  1.87 us (2%)
    pallas_call x1, Pallas kernels, on_device(): pl.pallas_call(functools.partial(kernel, nz, nx, ny, panels, width), out_...  81.1 us
    unnamed x1, local copies, waits for them, and re-layouts  1.87 us

profile of v4, /device:TPU:1, one launch (start us, length us, event | category | flops | bytes accessed | tf_op | source)
XLA Modules:
  0.0 83.0 jit_solution(2896211012328305137)
XLA Ops:
  0.0 81.1 %shard_map.55 = f32[512,256]{1,0:T(8,128)} custom-call(s32[4]{0:T(128)} %pivots.1, s32[4,32]{1,0:T(4,128)} %row_mask.1, s32[4,32]{1,0:T(4,128)} %col_mask.1, f32[2,32,8,256]{3,2,1,0:T(8,128)} %bitcast.2, f32[4,2,8,256]{3,2,1,0:T(8,128)} %bitcast.3), custom_call_target="tpu_custom_call" | custom-call | tf_op jit(solution)/shard_map/pallas_call | solution.py:435
  81.1 1.9 %copy.7 = f32[512,256]{1,0:T(8,128)} copy(f32[512,256]{1,0:T(8,128)} %shard_map.55) | data formatting | bytes 1048576
